TPU v7x, 128 devices: a whole 4x4x4 slice. The times are simulated.
128 devices in a mesh: mesh: 32 (over z, x, core), vec: 4 (over y).
Axes of the slice: x: 4, y: 4, z: 4, core: 2. Of those that a mesh axis runs over, the one named last changes fastest.
Arguments:
- panel: float32 [262144, 128], P('mesh', 'vec'), may hold values from -6 to 6
- orient: int32 [262144], P('mesh'), may hold values from -1 to 1, as said below
- mass: float32 [262144], P('mesh'), may hold values from 0.5 to 2
- stiff_diag: bfloat16 [2048, 128, 128], P('mesh'), may hold values from -0.05 to 4, as said below
- near_coupling: bfloat16 [2048, 128, 128], P('mesh'), may hold values from -0.1796875 to 0.1796875
- far_coupling: bfloat16 [2048, 128, 128], P('mesh'), may hold values from -0.1796875 to 0.1796875
Outputs:
- filtered: float32 [262144, 128], P('mesh', 'vec')
- ritz_stiff: float32 [128, 128], P('vec', 'mesh')
- ritz_mass: float32 [128, 128], P('vec', 'mesh')
Inputs may be any that keep to these rules, and one draw needn't show every extreme that they name: `orient`: every entry is +1 or -1. `stiff_diag`: each block is symmetric; its diagonal entries lie from 2 to 4 and its off-diagonal entries have magnitude at most 0.05.
All inputs are finite; a program needn't handle non-finite values.
Results may differ from a plain program's by a relative error of at most 0.0035.
Values may be sent and summed in bfloat16 or wider, within the bound.
A program may use at most 64 MiB of HBM per device.

v0:
```python
import functools

import jax
import jax.numpy as jnp
from jax import lax
from jax.experimental import pallas as pl
from jax.experimental.pallas import tpu as pltpu
from jax.sharding import PartitionSpec as P

SPAN = 32
BS = 128
DEGREE = 4
APPS = 2
NOPS = DEGREE * APPS
CENTER = 6.0

HALF = SPAN
STEPS = 4
CH = HALF // STEPS

MESH = pl.DeviceIdType.MESH
NT = (((1,), (1,)), ((), ()))
NN = (((1,), (0,)), ((), ()))
F32 = jnp.float32
BF16 = jnp.bfloat16


def block_of(q):
    return HALF * (q // HALF) + (q % HALF + 1) % HALF


def place_of(b):
    return HALF * (b // HALF) + (b % HALF - 1) % HALF


def lanes(q, n=1):
    return slice(q * BS, (q + n) * BS)


def dot(a, b, dims):
    return lax.dot_general(a, b, dims, preferred_element_type=F32)


def pieces():
    runs = []
    for s in range(STEPS):
        count = CH if s < STEPS - 1 else CH - 1
        runs.append((s * CH, s * CH + 1, count))
    runs.append((HALF - 1, 0, 1))
    return runs


RUNS = pieces()
NRUN = len(RUNS)


def runs_of(s):
    return (s,) if s < STEPS - 1 else (s, s + 1)


def kernel(
    nm, nv,
    x_hbm, orient_hbm, mass_hbm, diag_hbm, near_hbm, far_hbm,
    out_hbm, stiff_ref, massg_ref,
    orient, mass, scale, diag, near, far,
    x, acc, u, halo_u, p_out, halo_p,
    f_out, g_out, f_all, g_all, q_buf, t_buf, r_buf, s_buf, r2_buf,
    vec_sem, x_sem, far_sem, mat_sem, o_sem,
    us_sem, ur_sem, ps_sem, pr_sem,
    fs_sem, fr_sem, gs_sem, gr_sem,
    ts_sem, tr_sem, s2_sem, r2_sem,
):
    m = lax.axis_index("mesh")
    v = lax.axis_index("vec")

    cp_or = pltpu.make_async_copy(orient_hbm, orient, vec_sem.at[0])
    cp_ma = pltpu.make_async_copy(mass_hbm, mass, vec_sem.at[1])
    cp_or.start()
    cp_ma.start()

    def x_copy(h, r):
        pos, blk, n = RUNS[r]
        return pltpu.make_async_copy(
            x_hbm.at[:, lanes(h * HALF + blk, n)],
            x.at[0, :, lanes(h * HALF + pos, n)],
            x_sem.at[h, r],
        )

    def far_copy(r):
        _, blk, n = RUNS[r]
        return pltpu.make_async_copy(far_hbm.at[pl.ds(blk, n)], far.at[pl.ds(blk, n)], far_sem.at[r])

    for r in range(NRUN):
        x_copy(0, r).start()
        x_copy(1, r).start()
        far_copy(r).start()

    mats = [
        pltpu.make_async_copy(far_hbm.at[pl.ds(HALF, HALF)], far.at[pl.ds(HALF, HALF)], mat_sem.at[0]),
        pltpu.make_async_copy(diag_hbm, diag, mat_sem.at[1]),
        pltpu.make_async_copy(near_hbm, near, mat_sem.at[2]),
    ]
    for c in mats:
        c.start()

    @pl.when(m == 0)
    def _():
        halo_u[...] = jnp.zeros_like(halo_u)

    @pl.when(m == nm - 1)
    def _():
        halo_p[...] = jnp.zeros_like(halo_p)

    barrier = pltpu.get_barrier_semaphore()

    def hello_mesh(d, carry):
        pl.semaphore_signal(barrier, inc=1, device_id=(lax.rem(m + d, nm), v), device_id_type=MESH)
        return carry

    lax.fori_loop(1, nm, hello_mesh, 0)
    for d in range(1, nv):
        pl.semaphore_signal(barrier, inc=1, device_id=(m, lax.rem(v + d, nv)), device_id_type=MESH)

    cp_or.wait()
    cp_ma.wait()
    scale[...] = orient[...].astype(F32) / jnp.sqrt(mass[...])

    pl.semaphore_wait(barrier, nm - 1 + nv - 1)

    def send_u(par, s):
        return pltpu.make_async_remote_copy(
            src_ref=u.at[:, lanes(HALF + s * CH, CH)],
            dst_ref=halo_u.at[par, :, lanes(s * CH, CH)],
            send_sem=us_sem.at[s],
            recv_sem=ur_sem.at[par, s],
            device_id=(m + 1, v),
            device_id_type=MESH,
        )

    def send_p(par, s):
        n = CH + (s == STEPS - 1)
        return pltpu.make_async_remote_copy(
            src_ref=p_out.at[:, lanes(s * CH, n)],
            dst_ref=halo_p.at[par, :, lanes(s * CH, n)],
            send_sem=ps_sem.at[s],
            recv_sem=pr_sem.at[par, s],
            device_id=(m - 1, v),
            device_id_type=MESH,
        )

    def start_u(par, s):
        @pl.when(m < nm - 1)
        def _():
            send_u(par, s).start()

    def start_p(par, s):
        @pl.when(m > 0)
        def _():
            send_p(par, s).start()

    def wait_halo(par, s, sends=True):
        @pl.when(m > 0)
        def _():
            send_u(par, s).wait_recv()
            send_p(par, s).wait_send()

        @pl.when(m < nm - 1)
        def _():
            send_p(par, s).wait_recv()
            send_u(par, s).wait_send()

    def row_scale(q):
        b = block_of(q)
        return scale[b : b + 1, :]

    def products_down(s):
        for p in range(s * CH, (s + 1) * CH):
            b = block_of(p)
            up = u[:, lanes(p)]
            p_out[:, lanes(p)] = dot(up, far[b], NN).astype(BF16)
            if b == 0:
                p_out[:, lanes(HALF)] = dot(up, near[0], NN).astype(BF16)

    def local_terms(q):
        b = block_of(q)
        at = lambda c: u[:, lanes(place_of(c))]
        if b < HALF:
            if b > 0:
                total = dot(
                    jnp.concatenate([at(b - 1), at(b)], axis=1),
                    jnp.concatenate([near[b], diag[b]], axis=1), NT)
            else:
                total = dot(at(b), diag[b], NT)
            total += dot(
                jnp.concatenate([at(b + 1), at(b + HALF)], axis=1),
                jnp.concatenate([near[b + 1], far[b + HALF]], axis=0), NN)
        else:
            total = dot(
                jnp.concatenate([at(b - 1), at(b - HALF)], axis=1),
                jnp.concatenate([near[b], far[b]], axis=1), NT)
            if b < 2 * HALF - 1:
                total += dot(
                    jnp.concatenate([at(b), at(b + 1)], axis=1),
                    jnp.concatenate([diag[b], near[b + 1]], axis=0), NN)
            else:
                total += dot(at(b), diag[b], NN)
        acc[:, lanes(q)] = total

    def local_places(s):
        if s == 0:
            places = range(1, CH - 1)
        elif s < STEPS - 1:
            places = range(s * CH - 1, (s + 1) * CH - 1)
        else:
            places = [*range(s * CH - 1, HALF), 0]
        return places

    def local_step(s):
        for p in local_places(s):
            local_terms(p)
            local_terms(HALF + p)

    def upper_total(par, q):
        p = q - HALF
        total = acc[:, lanes(q)] + halo_p[par, :, lanes(p)].astype(F32)
        if block_of(q) == 2 * HALF - 1:
            total += halo_p[par, :, lanes(HALF)].astype(F32)
        return total

    def lower_total(par, p):
        b = block_of(p)
        if b == 0:
            far_term = dot(
                jnp.concatenate([halo_u[par, :, lanes(p)], halo_u[par, :, lanes(p - 1)]], axis=1),
                jnp.concatenate([far[b], near[b]], axis=1), NT)
        else:
            far_term = dot(halo_u[par, :, lanes(p)], far[b], NT)
        return acc[:, lanes(p)] + far_term

    def recur(q, total, now, weight, fresh):
        image = row_scale(q) * total
        current = x[now, :, lanes(q)]
        before = x[1 - now, :, lanes(q)]
        following = weight * (image - CENTER * current) - jnp.where(fresh, 0.0, before)
        x[1 - now, :, lanes(q)] = following
        u[:, lanes(q)] = (row_scale(q) * following).astype(BF16)
        return following

    def deal(q, value, box):
        p = q % HALF
        s, r = p // CH, p % CH
        per = CH // nv
        box[s, r // per, :, lanes((q // HALF) * per + r % per)] = value.astype(BF16)

    def exchange(box, whole, ss, rs, s, d):
        to = lax.rem(v + d, nv)
        return pltpu.make_async_remote_copy(
            src_ref=box.at[s, to],
            dst_ref=whole.at[s, pl.ds(pl.multiple_of(32 * v, 32), 32), :],
            send_sem=ss.at[d - 1, s],
            recv_sem=rs.at[d - 1, s],
            device_id=(m, to),
            device_id_type=MESH,
        )

    def spread(box, whole, ss, rs, s):
        for d in (2, 1, 3):
            exchange(box, whole, ss, rs, s, d).start()
        whole[s, pl.ds(pl.multiple_of(32 * v, 32), 32), :] = box[s, v]

    def out_copy(h, r):
        pos, blk, n = RUNS[r]
        return pltpu.make_async_copy(
            x.at[0, :, lanes(h * HALF + pos, n)],
            out_hbm.at[:, lanes(h * HALF + blk, n)],
            o_sem.at[h, r],
        )

    for s in range(STEPS):
        for r in runs_of(s):
            x_copy(1, r).wait()
        for q in range(HALF + s * CH, HALF + (s + 1) * CH):
            u[:, lanes(q)] = (row_scale(q) * x[0, :, lanes(q)]).astype(BF16)
        start_u(0, s)
        for r in runs_of(s):
            x_copy(0, r).wait()
            far_copy(r).wait()
        for p in range(s * CH, (s + 1) * CH):
            u[:, lanes(p)] = (row_scale(p) * x[0, :, lanes(p)]).astype(BF16)
        if s == STEPS - 1:
            mats[2].wait()
        products_down(s)
        start_p(0, s)
    mats[0].wait()
    mats[1].wait()
    for s in range(STEPS):
        local_step(s)

    def operation(k, last):
        par = lax.rem(k, 2)
        nxt = 1 - par
        fresh = lax.rem(k, DEGREE) == 0
        weight = jnp.where(fresh, 0.125, 0.25).astype(F32)
        for s in range(STEPS):
            wait_halo(par, s)
            for q in range(HALF + s * CH, HALF + (s + 1) * CH):
                value = recur(q, upper_total(par, q), par, weight, fresh)
                if last:
                    deal(q, value, f_out)
            start_u(nxt, s)
            for p in range(s * CH, (s + 1) * CH):
                value = recur(p, lower_total(par, p), par, weight, fresh)
                if last:
                    deal(p, value, f_out)
            products_down(s)
            start_p(nxt, s)
            if last:
                spread(f_out, f_all, fs_sem, fr_sem, s)
                for r in runs_of(s):
                    out_copy(0, r).start()
                    out_copy(1, r).start()
            local_step(s)

    def loop_body(k, carry):
        operation(k, False)
        return carry

    lax.fori_loop(0, NOPS - 1, loop_body, 0)
    operation(NOPS - 1, True)

    for s in range(STEPS):
        wait_halo(NOPS % 2, s)
        for q in range(HALF + s * CH, HALF + (s + 1) * CH):
            deal(q, row_scale(q) * upper_total(NOPS % 2, q), g_out)
        for p in range(s * CH, (s + 1) * CH):
            deal(p, row_scale(p) * lower_total(NOPS % 2, p), g_out)
        spread(g_out, g_all, gs_sem, gr_sem, s)

    for s in range(STEPS):
        for d in range(1, nv):
            exchange(f_out, f_all, fs_sem, fr_sem, s, d).wait()
        part = dot(f_all[s], f_all[s], NT)
        q_buf[1] = part if s == 0 else q_buf[1] + part
    for s in range(STEPS):
        for d in range(1, nv):
            exchange(g_out, g_all, gs_sem, gr_sem, s, d).wait()
        part = dot(g_all[s], f_all[s], NT)
        q_buf[0] = part if s == 0 else q_buf[0] + part

    width = 128 // nm
    for i in range(nm):
        t_buf[i, 0:width, :] = q_buf[0, i * width : (i + 1) * width, :]
        t_buf[i, width : 2 * width, :] = q_buf[1, i * width : (i + 1) * width, :]

    def fold(d):
        to = lax.rem(m + d, nm)
        return pltpu.make_async_remote_copy(
            src_ref=t_buf.at[to],
            dst_ref=r_buf.at[d - 1],
            send_sem=ts_sem.at[d - 1],
            recv_sem=tr_sem.at[d - 1],
            device_id=(to, v),
            device_id_type=MESH,
        )

    def fold_start(d, carry):
        fold(d).start()
        return carry

    def fold_wait(d, carry):
        fold(d).wait()
        return carry + r_buf[d - 1]

    lax.fori_loop(1, nm, fold_start, 0)
    s_buf[...] = lax.fori_loop(1, nm, fold_wait, t_buf[m])

    def fold_vec(d):
        return pltpu.make_async_remote_copy(
            src_ref=s_buf,
            dst_ref=r2_buf.at[d - 1],
            send_sem=s2_sem.at[d - 1],
            recv_sem=r2_sem.at[d - 1],
            device_id=(m, lax.rem(v + d, nv)),
            device_id_type=MESH,
        )

    for d in range(1, nv):
        fold_vec(d).start()
    total = s_buf[...]
    for d in range(1, nv):
        fold_vec(d).wait()
        total = total + r2_buf[d - 1]
    cols = 128 // nv
    mine = jnp.zeros((2 * width, cols), F32)
    for j in range(nv):
        mine = jnp.where(v == j, total[:, j * cols : (j + 1) * cols], mine)
    stiff_ref[...] = mine[0:width]
    massg_ref[...] = mine[width : 2 * width]

    for h in range(2):
        for r in range(NRUN):
            out_copy(h, r).wait()


def shards(nm, nv, panel, orient, mass, stiff_diag, near_coupling, far_coupling):
    rows, columns = panel.shape
    blocks = stiff_diag.shape[0]
    width = 128 // nm
    anywhere = pl.BlockSpec(memory_space=pl.ANY)
    inside = pl.BlockSpec(memory_space=pltpu.VMEM)
    dma = pltpu.SemaphoreType.DMA
    mat = pltpu.VMEM((blocks, BS, BS), BF16)
    scratch = [
        pltpu.VMEM((blocks, BS), jnp.int32),
        pltpu.VMEM((blocks, BS), F32),
        pltpu.VMEM((blocks, BS), F32),
        mat, mat, mat,
        pltpu.VMEM((2, columns, rows), F32),
        pltpu.VMEM((columns, rows), F32),
        pltpu.VMEM((columns, rows), BF16),
        pltpu.VMEM((2, columns, HALF * BS), BF16),
        pltpu.VMEM((columns, (HALF + 1) * BS), BF16),
        pltpu.VMEM((2, columns, (HALF + 1) * BS), BF16),
        pltpu.VMEM((STEPS, nv, columns, rows // STEPS // nv), BF16),
        pltpu.VMEM((STEPS, nv, columns, rows // STEPS // nv), BF16),
        pltpu.VMEM((STEPS, nv * columns, rows // STEPS // nv), BF16),
        pltpu.VMEM((STEPS, nv * columns, rows // STEPS // nv), BF16),
        pltpu.VMEM((2, 128, 128), F32),
        pltpu.VMEM((nm, 2 * width, 128), F32),
        pltpu.VMEM((nm - 1, 2 * width, 128), F32),
        pltpu.VMEM((2 * width, 128), F32),
        pltpu.VMEM((nv - 1, 2 * width, 128), F32),
        dma((2,)), dma((2, NRUN)), dma((NRUN,)), dma((3,)), dma((2, NRUN)),
        dma((STEPS,)), dma((2, STEPS)), dma((STEPS,)), dma((2, STEPS)),
        dma((nv - 1, STEPS)), dma((nv - 1, STEPS)), dma((nv - 1, STEPS)), dma((nv - 1, STEPS)),
        dma((nm - 1,)), dma((nm - 1,)), dma((nv - 1,)), dma((nv - 1,)),
    ]
    filtered, stiff, massg = pl.pallas_call(
        functools.partial(kernel, nm, nv),
        out_shape=(
            jax.ShapeDtypeStruct((columns, rows), F32),
            jax.ShapeDtypeStruct((width, 128 // nv), F32),
            jax.ShapeDtypeStruct((width, 128 // nv), F32),
        ),
        in_specs=[anywhere] * 6,
        out_specs=(anywhere, inside, inside),
        scratch_shapes=scratch,
        compiler_params=pltpu.CompilerParams(collective_id=0, has_side_effects=True),
        name="filter_ritz",
    )(
        panel.T,
        orient.reshape(blocks, BS),
        mass.reshape(blocks, BS),
        stiff_diag,
        near_coupling,
        far_coupling,
    )
    return (filtered.T, stiff.T, massg.T)


def solution(mesh):
    placed = (
        P("mesh", "vec"),
        P("mesh"),
        P("mesh"),
        P("mesh", None, None),
        P("mesh", None, None),
        P("mesh", None, None),
    )
    return jax.shard_map(
        functools.partial(shards, mesh.shape["mesh"], mesh.shape["vec"]),
        mesh=mesh,
        in_specs=placed,
        out_specs=(P("mesh", "vec"), P("vec", "mesh"), P("vec", "mesh")),
        check_vma=False,
    )
```

profile of v0, /device:TPU:1, one launch (start us, length us, event | category | flops | bytes accessed | tf_op | source)
XLA Modules:
  0.0 70.2 jit_solution(12954352943918837963)
XLA Ops:
  0.6 66.1 %filter_ritz.1 = (f32[32,8192]{1,0:T(8,128)}, f32[4,32]{1,0:T(4,128)}, f32[4,32]{1,0:T(4,128)}) custom-call(f32[32,8192]{1,0:T(8,128)} %bitcast.6, s32[64,128]{1,0:T(8,128)} %bitcast.8, f32[64,128]{1,0:T(8,128)} %bitcast.9, bf16[64,128,128]{2,1,0:T(8,128)(2,1)} %diag_hbm.1, bf16[64,128,128]{2,1,0:T(8,128)(2,1)} %near_hbm.1, bf16[64,128,128]{2,1,0:T(8,128)(2,1)} %far_hbm.1), custom_call_target="tpu_custom_call" | custom-call | tf_op jit(solution)/shard_map/filter_ritz/pallas_call | solution.py:438
  66.8 0.0 copy-start.1
  66.8 0.0 copy-start
  66.8 2.3 %copy.12 = f32[8192,32]{0,1:T(8,128)} copy(f32[8192,32]{0,1:T(8,128)} %bitcast.7) | data formatting | bytes 2097152
  69.0 0.0 copy-done.1
  69.0 0.6 copy.13
  69.6 0.0 copy-done
  69.6 0.6 copy.14
Async XLA Ops:
  66.8 2.3 %copy-start.1 = (f32[4,32]{1,0:T(4,128)S(1)}, f32[4,32]{1,0:T(4,128)}, u32[]{:S(2)}) copy-start(f32[4,32]{1,0:T(4,128)} %get-tuple-element.7) | copy-start | bytes 1540
  66.8 2.9 %copy-start = (f32[4,32]{1,0:T(4,128)S(1)}, f32[4,32]{1,0:T(4,128)}, u32[]{:S(2)}) copy-start(f32[4,32]{1,0:T(4,128)} %get-tuple-element.8) | copy-start | bytes 1540
where the time goes:
time: 70.3 us; the launch traced here: 70.2 us
  Pallas kernels  66.1 us (94%)
  local copies, waits for them, and re-layouts  3.43 us (5%)
    pallas_call x1, Pallas kernels, shards(): pl.pallas_call(functools.partial(kernel, nm, nv), out_shape=(jax.ShapeDty...  66.1 us
    unnamed x7, local copies, waits for them, and re-layouts  3.43 us

commit v1 on v0

v1 whole, which is shorter than its diff:
```python
import functools

import jax
import jax.numpy as jnp
from jax import lax
from jax.experimental import pallas as pl
from jax.experimental.pallas import tpu as pltpu
from jax.sharding import PartitionSpec as P

SPAN = 32
BS = 128
DEGREE = 4
APPS = 2
NOPS = DEGREE * APPS
CENTER = 6.0

HALF = SPAN
STEPS = 4
CH = HALF // STEPS
GROUP = 8
VMEM_LIMIT = 32 * 1024 * 1024

MESH = pl.DeviceIdType.MESH
NT = (((1,), (1,)), ((), ()))
NN = (((1,), (0,)), ((), ()))
F32 = jnp.float32
BF16 = jnp.bfloat16


def block_of(q):
    return HALF * (q // HALF) + (q % HALF + 1) % HALF


def place_of(b):
    return HALF * (b // HALF) + (b % HALF - 1) % HALF


def lanes(q, n=1):
    return slice(q * BS, (q + n) * BS)


def dot(a, b, dims):
    return lax.dot_general(a, b, dims, preferred_element_type=F32)


def pieces():
    runs = []
    for s in range(STEPS):
        count = CH if s < STEPS - 1 else CH - 1
        runs.append((s * CH, s * CH + 1, count))
    runs.append((HALF - 1, 0, 1))
    return runs


RUNS = pieces()
NRUN = len(RUNS)


def runs_of(s):
    return (s,) if s < STEPS - 1 else (s, s + 1)


def kernel(
    nm, nv,
    x_hbm, orient_hbm, mass_hbm, diag_hbm, near_hbm, far_hbm,
    out_hbm, ritz_ref,
    orient, mass, scale, pair, side, far,
    x, acc, u, halo_u, p_out, halo_p,
    f_out, g_out, f_all, g_all, q_buf, t_buf, ra_buf, sa_buf, rb_buf, sb_buf, rc_buf,
    vec_sem, x_sem, far_sem, mat_sem, o_sem,
    us_sem, ur_sem, ps_sem, pr_sem,
    fs_sem, fr_sem, gs_sem, gr_sem,
    as_sem, ar_sem, bs_sem, br_sem, cs_sem, cr_sem,
):
    m = lax.axis_index("mesh")
    v = lax.axis_index("vec")

    cp_or = pltpu.make_async_copy(orient_hbm, orient, vec_sem.at[0])
    cp_ma = pltpu.make_async_copy(mass_hbm, mass, vec_sem.at[1])
    cp_or.start()
    cp_ma.start()

    def x_copy(h, r):
        pos, blk, n = RUNS[r]
        return pltpu.make_async_copy(
            x_hbm.at[:, lanes(h * HALF + blk, n)],
            x.at[0, :, lanes(h * HALF + pos, n)],
            x_sem.at[h, r],
        )

    def far_copy(r):
        _, blk, n = RUNS[r]
        return pltpu.make_async_copy(far_hbm.at[pl.ds(blk, n)], far.at[pl.ds(blk, n)], far_sem.at[r])

    for r in range(NRUN):
        x_copy(0, r).start()
        x_copy(1, r).start()
        far_copy(r).start()

    lo, hi = pl.ds(0, BS), pl.ds(BS, BS)
    first, second = pl.ds(0, HALF), pl.ds(HALF, HALF)
    mats = [
        pltpu.make_async_copy(near_hbm, side.at[:, :, lo], mat_sem.at[0]),
        pltpu.make_async_copy(far_hbm.at[second], pair.at[:, hi, lo], mat_sem.at[1]),
        pltpu.make_async_copy(diag_hbm.at[first], pair.at[:, lo, lo], mat_sem.at[2]),
        pltpu.make_async_copy(diag_hbm.at[second], pair.at[:, hi, hi], mat_sem.at[3]),
    ]
    for c in mats:
        c.start()

    group = lax.div(m, GROUP)
    member = lax.rem(m, GROUP)
    ngroup = nm // GROUP
    up, down = lax.rem(m + 1, nm), lax.rem(m + nm - 1, nm)

    def in_group(d):
        return group * GROUP + lax.rem(member + d, GROUP)

    def in_column(d):
        return lax.rem(group + d, ngroup) * GROUP + member

    barrier = pltpu.get_barrier_semaphore()
    greeted = [(up, v), (down, v)]
    greeted += [(in_group(d), v) for d in range(1, GROUP)]
    greeted += [(in_column(d), v) for d in range(1, ngroup)]
    greeted += [(m, lax.rem(v + d, nv)) for d in range(1, nv)]
    for peer in greeted:
        pl.semaphore_signal(barrier, inc=1, device_id=peer, device_id_type=MESH)

    cp_or.wait()
    cp_ma.wait()
    scale[...] = orient[...].astype(F32) / jnp.sqrt(mass[...])

    pl.semaphore_wait(barrier, len(greeted))

    def send_u(par, s):
        return pltpu.make_async_remote_copy(
            src_ref=u.at[:, lanes(HALF + s * CH, CH)],
            dst_ref=halo_u.at[par, :, lanes(s * CH, CH)],
            send_sem=us_sem.at[s],
            recv_sem=ur_sem.at[par, s],
            device_id=(up, v),
            device_id_type=MESH,
        )

    def send_p(par, s):
        n = CH + (s == STEPS - 1)
        return pltpu.make_async_remote_copy(
            src_ref=p_out.at[:, lanes(s * CH, n)],
            dst_ref=halo_p.at[par, :, lanes(s * CH, n)],
            send_sem=ps_sem.at[s],
            recv_sem=pr_sem.at[par, s],
            device_id=(down, v),
            device_id_type=MESH,
        )

    def wait_halo(par, s):
        send_u(par, s).wait()
        send_p(par, s).wait()

    has_below = m > 0
    has_above = m < nm - 1

    def row_scale(q):
        b = block_of(q)
        return scale[b : b + 1, :]

    def products_down(s):
        for p in range(s * CH, (s + 1) * CH):
            b = block_of(p)
            mine = u[:, lanes(p)]
            p_out[:, lanes(p)] = dot(mine, far[b], NN).astype(BF16)
            if b == 0:
                p_out[:, lanes(HALF)] = dot(mine, side[0, :, 0:BS], NN).astype(BF16)

    def local_step(s, done, waiting):
        def give(q, value):
            if q in done:
                acc[:, lanes(q)] += value
            elif q in waiting:
                waiting[q] += value
            else:
                waiting[q] = value

        own = []
        for p in range(s * CH, (s + 1) * CH):
            b = block_of(p)
            both = dot(jnp.concatenate([u[:, lanes(p)], u[:, lanes(HALF + p)]], axis=1), pair[b], NN)
            give(p, both[:, 0:BS])
            give(HALF + p, both[:, BS : 2 * BS])
            own += [p, HALF + p]
            for q in (p, HALF + p):
                b = block_of(q)
                beside = dot(u[:, lanes(q)], side[b], NN)
                if b > 0:
                    give(place_of(b - 1), beside[:, 0:BS])
                if b < 2 * HALF - 1:
                    give(place_of(b + 1), beside[:, BS : 2 * BS])
        for q in own:
            acc[:, lanes(q)] = waiting.pop(q)
            done.add(q)

    def local_all():
        done, waiting = set(), {}
        for s in range(STEPS):
            yield functools.partial(local_step, s, done, waiting)

    def upper_total(par, q):
        p = q - HALF
        other = halo_p[par, :, lanes(p)].astype(F32)
        if block_of(q) == 2 * HALF - 1:
            other += halo_p[par, :, lanes(HALF)].astype(F32)
        return acc[:, lanes(q)] + jnp.where(has_above, other, 0.0)

    def lower_total(par, p):
        b = block_of(p)
        if b == 0:
            far_term = dot(
                jnp.concatenate([halo_u[par, :, lanes(p)], halo_u[par, :, lanes(p - 1)]], axis=1),
                jnp.concatenate([far[b], side[b, :, 0:BS]], axis=1), NT)
        else:
            far_term = dot(halo_u[par, :, lanes(p)], far[b], NT)
        return acc[:, lanes(p)] + jnp.where(has_below, far_term, 0.0)

    def recur(q, total, now, weight, fresh):
        image = row_scale(q) * total
        current = x[now, :, lanes(q)]
        before = x[1 - now, :, lanes(q)]
        following = weight * (image - CENTER * current) - jnp.where(fresh, 0.0, before)
        x[1 - now, :, lanes(q)] = following
        u[:, lanes(q)] = (row_scale(q) * following).astype(BF16)
        return following

    def deal(q, value, box):
        p = q % HALF
        s, r = p // CH, p % CH
        per = CH // nv
        box[s, r // per, :, lanes((q // HALF) * per + r % per)] = value.astype(BF16)

    def exchange(box, whole, ss, rs, s, d):
        to = lax.rem(v + d, nv)
        return pltpu.make_async_remote_copy(
            src_ref=box.at[s, to],
            dst_ref=whole.at[s, pl.ds(pl.multiple_of(32 * v, 32), 32), :],
            send_sem=ss.at[d - 1, s],
            recv_sem=rs.at[d - 1, s],
            device_id=(m, to),
            device_id_type=MESH,
        )

    def spread(box, whole, ss, rs, s):
        for d in (2, 1, 3):
            exchange(box, whole, ss, rs, s, d).start()
        whole[s, pl.ds(pl.multiple_of(32 * v, 32), 32), :] = box[s, v]

    def out_copy(h, r):
        pos, blk, n = RUNS[r]
        return pltpu.make_async_copy(
            x.at[0, :, lanes(h * HALF + pos, n)],
            out_hbm.at[:, lanes(h * HALF + blk, n)],
            o_sem.at[h, r],
        )

    for s in range(STEPS):
        for r in runs_of(s):
            x_copy(1, r).wait()
        for q in range(HALF + s * CH, HALF + (s + 1) * CH):
            u[:, lanes(q)] = (row_scale(q) * x[0, :, lanes(q)]).astype(BF16)
        send_u(0, s).start()
        for r in runs_of(s):
            x_copy(0, r).wait()
            far_copy(r).wait()
        for p in range(s * CH, (s + 1) * CH):
            u[:, lanes(p)] = (row_scale(p) * x[0, :, lanes(p)]).astype(BF16)
        if s == STEPS - 1:
            mats[0].wait()
        products_down(s)
        send_p(0, s).start()
    for c in mats[1:]:
        c.wait()

    def turn(b, carry):
        pair[b, 0:BS, BS : 2 * BS] = pair[b, BS : 2 * BS, 0:BS].T
        side[2 * b, :, BS : 2 * BS] = side[2 * b + 1, :, 0:BS].T
        side[2 * b + 1, :, BS : 2 * BS] = side[jnp.minimum(2 * b + 2, 2 * HALF - 1), :, 0:BS].T
        return carry

    lax.fori_loop(0, HALF, turn, 0, unroll=2)
    for step in local_all():
        step()

    def operation(k, last):
        par = lax.rem(k, 2)
        nxt = 1 - par
        fresh = lax.rem(k, DEGREE) == 0
        weight = jnp.where(fresh, 0.125, 0.25).astype(F32)
        local = list(local_all())
        for s in range(STEPS):
            wait_halo(par, s)
            for q in range(HALF + s * CH, HALF + (s + 1) * CH):
                value = recur(q, upper_total(par, q), par, weight, fresh)
                if last:
                    deal(q, value, f_out)
            send_u(nxt, s).start()
            for p in range(s * CH, (s + 1) * CH):
                value = recur(p, lower_total(par, p), par, weight, fresh)
                if last:
                    deal(p, value, f_out)
            products_down(s)
            send_p(nxt, s).start()
            if last:
                spread(f_out, f_all, fs_sem, fr_sem, s)
                for r in runs_of(s):
                    out_copy(0, r).start()
                    out_copy(1, r).start()
            local[s]()

    def loop_body(k, carry):
        operation(k, False)
        return carry

    lax.fori_loop(0, NOPS - 1, loop_body, 0)
    operation(NOPS - 1, True)

    for s in range(STEPS):
        wait_halo(NOPS % 2, s)
        for q in range(HALF + s * CH, HALF + (s + 1) * CH):
            deal(q, row_scale(q) * upper_total(NOPS % 2, q), g_out)
        for p in range(s * CH, (s + 1) * CH):
            deal(p, row_scale(p) * lower_total(NOPS % 2, p), g_out)
        spread(g_out, g_all, gs_sem, gr_sem, s)

    for s in range(STEPS):
        for d in range(1, nv):
            exchange(f_out, f_all, fs_sem, fr_sem, s, d).wait()
        part = dot(f_all[s], f_all[s], NT)
        q_buf[1] = part if s == 0 else q_buf[1] + part
    for s in range(STEPS):
        for d in range(1, nv):
            exchange(g_out, g_all, gs_sem, gr_sem, s, d).wait()
        part = dot(g_all[s], f_all[s], NT)
        q_buf[0] = part if s == 0 else q_buf[0] + part

    width = 128 // nm
    for i in range(nm):
        t_buf[i % GROUP, i // GROUP, 0:width, :] = q_buf[0, i * width : (i + 1) * width, :]
        t_buf[i % GROUP, i // GROUP, width : 2 * width, :] = q_buf[1, i * width : (i + 1) * width, :]

    def fold(source, box, ss, rs, d, peer):
        return pltpu.make_async_remote_copy(
            src_ref=source, dst_ref=box.at[d - 1], send_sem=ss.at[d - 1], recv_sem=rs.at[d - 1],
            device_id=peer, device_id_type=MESH)

    def fold_a(d):
        return fold(t_buf.at[lax.rem(member + d, GROUP)], ra_buf, as_sem, ar_sem, d, (in_group(d), v))

    def fold_b(d):
        return fold(sa_buf.at[lax.rem(group + d, ngroup)], rb_buf, bs_sem, br_sem, d, (in_column(d), v))

    def fold_c(d):
        return fold(sb_buf, rc_buf, cs_sem, cr_sem, d, (m, lax.rem(v + d, nv)))

    for d in range(1, GROUP):
        fold_a(d).start()
    total = t_buf[member]
    for d in range(1, GROUP):
        fold_a(d).wait()
        total = total + ra_buf[d - 1]
    sa_buf[...] = total
    for d in range(1, ngroup):
        fold_b(d).start()
    total = sa_buf[group]
    for d in range(1, ngroup):
        fold_b(d).wait()
        total = total + rb_buf[d - 1]
    sb_buf[...] = total
    for d in range(1, nv):
        fold_c(d).start()
    for d in range(1, nv):
        fold_c(d).wait()
        total = total + rc_buf[d - 1]
    cols = 128 // nv
    mine = jnp.zeros((2 * width, cols), F32)
    for j in range(nv):
        mine = jnp.where(v == j, total[:, j * cols : (j + 1) * cols], mine)
    ritz_ref[...] = mine

    for h in range(2):
        for r in range(NRUN):
            out_copy(h, r).wait()


def write_out(filtered, ritz, out, stiff, massg, sem):
    copy = pltpu.make_async_copy(filtered, out, sem)
    copy.start()
    width = stiff.shape[0]
    stiff[...] = ritz[0:width]
    massg[...] = ritz[width : 2 * width]
    copy.wait()


def shards(nm, nv, panel, orient, mass, stiff_diag, near_coupling, far_coupling):
    rows, columns = panel.shape
    blocks = stiff_diag.shape[0]
    width = 128 // nm
    cols = 128 // nv
    ngroup = nm // GROUP
    anywhere = pl.BlockSpec(memory_space=pl.ANY)
    inside = pl.BlockSpec(memory_space=pltpu.VMEM)
    dma = pltpu.SemaphoreType.DMA
    dealt = rows // STEPS // nv
    scratch = [
        pltpu.VMEM((blocks, BS), jnp.int32),
        pltpu.VMEM((blocks, BS), F32),
        pltpu.VMEM((blocks, BS), F32),
        pltpu.VMEM((HALF, 2 * BS, 2 * BS), BF16),
        pltpu.VMEM((blocks, BS, 2 * BS), BF16),
        pltpu.VMEM((HALF, BS, BS), BF16),
        pltpu.VMEM((2, columns, rows), F32),
        pltpu.VMEM((columns, rows), F32),
        pltpu.VMEM((columns, rows), BF16),
        pltpu.VMEM((2, columns, HALF * BS), BF16),
        pltpu.VMEM((columns, (HALF + 1) * BS), BF16),
        pltpu.VMEM((2, columns, (HALF + 1) * BS), BF16),
        pltpu.VMEM((STEPS, nv, columns, dealt), BF16),
        pltpu.VMEM((STEPS, nv, columns, dealt), BF16),
        pltpu.VMEM((STEPS, nv * columns, dealt), BF16),
        pltpu.VMEM((STEPS, nv * columns, dealt), BF16),
        pltpu.VMEM((2, 128, 128), F32),
        pltpu.VMEM((GROUP, ngroup, 2 * width, 128), F32),
        pltpu.VMEM((GROUP - 1, ngroup, 2 * width, 128), F32),
        pltpu.VMEM((ngroup, 2 * width, 128), F32),
        pltpu.VMEM((ngroup - 1, 2 * width, 128), F32),
        pltpu.VMEM((2 * width, 128), F32),
        pltpu.VMEM((nv - 1, 2 * width, 128), F32),
        dma((2,)), dma((2, NRUN)), dma((NRUN,)), dma((4,)), dma((2, NRUN)),
        dma((STEPS,)), dma((2, STEPS)), dma((STEPS,)), dma((2, STEPS)),
        dma((nv - 1, STEPS)), dma((nv - 1, STEPS)), dma((nv - 1, STEPS)), dma((nv - 1, STEPS)),
        dma((GROUP - 1,)), dma((GROUP - 1,)), dma((ngroup - 1,)), dma((ngroup - 1,)), dma((nv - 1,)), dma((nv - 1,)),
    ]
    filtered, ritz = pl.pallas_call(
        functools.partial(kernel, nm, nv),
        out_shape=(
            jax.ShapeDtypeStruct((columns, rows), F32),
            jax.ShapeDtypeStruct((2 * width, cols), F32),
        ),
        in_specs=[pl.BlockSpec(memory_space=pltpu.HBM)] * 6,
        out_specs=(anywhere, inside),
        scratch_shapes=scratch,
        compiler_params=pltpu.CompilerParams(
            collective_id=0, has_side_effects=True, vmem_limit_bytes=VMEM_LIMIT),
        name="filter_ritz",
    )(*[
        pltpu.with_memory_space_constraint(a, pltpu.HBM)
        for a in (
            panel.T,
            orient.reshape(blocks, BS),
            mass.reshape(blocks, BS),
            stiff_diag,
            near_coupling,
            far_coupling,
        )
    ])
    filtered, stiff, massg = pl.pallas_call(
        write_out,
        out_shape=(
            jax.ShapeDtypeStruct((columns, rows), F32),
            jax.ShapeDtypeStruct((width, cols), F32),
            jax.ShapeDtypeStruct((width, cols), F32),
        ),
        in_specs=[inside, inside],
        out_specs=(anywhere, inside, inside),
        scratch_shapes=[pltpu.SemaphoreType.DMA],
        compiler_params=pltpu.CompilerParams(vmem_limit_bytes=VMEM_LIMIT),
        name="write_out",
    )(filtered, ritz)
    return (filtered.T, stiff.T, massg.T)


def solution(mesh):
    placed = (
        P("mesh", "vec"),
        P("mesh"),
        P("mesh"),
        P("mesh", None, None),
        P("mesh", None, None),
        P("mesh", None, None),
    )
    return jax.shard_map(
        functools.partial(shards, mesh.shape["mesh"], mesh.shape["vec"]),
        mesh=mesh,
        in_specs=placed,
        out_specs=(P("mesh", "vec"), P("vec", "mesh"), P("vec", "mesh")),
        check_vma=False,
    )
```

time: 70.3 us -> 71 us (level); the launches traced: 70.2 us -> 70.1 us
  local copies, waits for them, and re-layouts: 3.43 us -> 0 us
  Pallas kernels: 66.1 us -> 69.5 us
    unnamed x7 -> x0, local copies, waits for them, and re-layouts: 3.43 us -> none
    pallas_call x1, Pallas kernels: 66.1 us -> 67.9 us  [shards(): pl.pallas_call(functools.partial(kernel, nm, nv), out_shape=(jax.ShapeDty...]
    pallas_call x0 -> x1, Pallas kernels: none -> 1.56 us  [shards(): pl.pallas_call(write_out, out_shape=(jax.ShapeDtypeStruct((columns, rows)...]
where the time goes in v1:
time: 71 us; the launch traced here: 70.1 us
  Pallas kernels  69.5 us (98%)
    pallas_call x1, Pallas kernels, shards(): pl.pallas_call(functools.partial(kernel, nm, nv), out_shape=(jax.ShapeDty...  67.9 us
    pallas_call x1, Pallas kernels, shards(): pl.pallas_call(write_out, out_shape=(jax.ShapeDtypeStruct((columns, rows)...  1.56 us

profile of v1, /device:TPU:1, one launch (start us, length us, event | category | flops | bytes accessed | tf_op | source)
XLA Modules:
  0.0 70.1 jit_solution(14626389852652952612)
XLA Ops:
  0.6 67.9 %filter_ritz.1 = (f32[32,8192]{1,0:T(8,128)S(1)}, f32[8,32]{1,0:T(8,128)S(1)}) custom-call(f32[32,8192]{1,0:T(8,128)} %bitcast.6, s32[64,128]{1,0:T(8,128)} %bitcast.7, f32[64,128]{1,0:T(8,128)} %bitcast.8, bf16[64,128,128]{2,1,0:T(8,128)(2,1)} %diag_hbm.1, bf16[64,128,128]{2,1,0:T(8,128)(2,1)} %near_hbm.1, bf16[64,128,128]{2,1,0:T(8,128)(2,1)} %far_hbm.1), custom_call_target="tpu_custom_call" | custom-call | tf_op jit(solution)/shard_map/filter_ritz/pallas_call | solution.py:441
  68.6 1.6 %write_out.1 = (f32[32,8192]{1,0:T(8,128)}, f32[4,32]{1,0:T(4,128)}, f32[4,32]{1,0:T(4,128)}) custom-call(f32[32,8192]{1,0:T(8,128)S(1)} %get-tuple-element.8.filtered, f32[8,32]{1,0:T(8,128)S(1)} %get-tuple-element.9.ritz), custom_call_target="tpu_custom_call" | custom-call | tf_op jit(solution)/shard_map/write_out/pallas_call | solution.py:464

commit v2 on v0

--- a/solution.py
+++ b/solution.py
@@ -17,6 +17,7 @@
 HALF = SPAN
 STEPS = 4
 CH = HALF // STEPS
+VMEM_LIMIT = 32 * 1024 * 1024
 
 MESH = pl.DeviceIdType.MESH
 NT = (((1,), (1,)), ((), ()))
@@ -61,7 +62,7 @@
 def kernel(
     nm, nv,
     x_hbm, orient_hbm, mass_hbm, diag_hbm, near_hbm, far_hbm,
-    out_hbm, stiff_ref, massg_ref,
+    out_hbm, ritz_ref,
     orient, mass, scale, diag, near, far,
     x, acc, u, halo_u, p_out, halo_p,
     f_out, g_out, f_all, g_all, q_buf, t_buf, r_buf, s_buf, r2_buf,
@@ -307,12 +308,12 @@
                 value = recur(q, upper_total(par, q), par, weight, fresh)
                 if last:
                     deal(q, value, f_out)
-            start_u(nxt, s)
             for p in range(s * CH, (s + 1) * CH):
                 value = recur(p, lower_total(par, p), par, weight, fresh)
                 if last:
                     deal(p, value, f_out)
             products_down(s)
+            start_u(nxt, s)
             start_p(nxt, s)
             if last:
                 spread(f_out, f_all, fs_sem, fr_sem, s)
@@ -338,12 +339,12 @@
 
     for s in range(STEPS):
         for d in range(1, nv):
-            exchange(f_out, f_all, fs_sem, fr_sem, s, d).wait()
+            exchange(f_out, f_all, fs_sem, fr_sem, s, d).wait_recv()
         part = dot(f_all[s], f_all[s], NT)
         q_buf[1] = part if s == 0 else q_buf[1] + part
     for s in range(STEPS):
         for d in range(1, nv):
-            exchange(g_out, g_all, gs_sem, gr_sem, s, d).wait()
+            exchange(g_out, g_all, gs_sem, gr_sem, s, d).wait_recv()
         part = dot(g_all[s], f_all[s], NT)
         q_buf[0] = part if s == 0 else q_buf[0] + part
 
@@ -368,7 +369,7 @@
         return carry
 
     def fold_wait(d, carry):
-        fold(d).wait()
+        fold(d).wait_recv()
         return carry + r_buf[d - 1]
 
     lax.fori_loop(1, nm, fold_start, 0)
@@ -388,24 +389,45 @@
         fold_vec(d).start()
     total = s_buf[...]
     for d in range(1, nv):
-        fold_vec(d).wait()
+        fold_vec(d).wait_recv()
         total = total + r2_buf[d - 1]
     cols = 128 // nv
     mine = jnp.zeros((2 * width, cols), F32)
     for j in range(nv):
         mine = jnp.where(v == j, total[:, j * cols : (j + 1) * cols], mine)
-    stiff_ref[...] = mine[0:width]
-    massg_ref[...] = mine[width : 2 * width]
-
+    ritz_ref[...] = mine
+
+    for s in range(STEPS):
+        for d in range(1, nv):
+            exchange(f_out, f_all, fs_sem, fr_sem, s, d).wait_send()
+            exchange(g_out, g_all, gs_sem, gr_sem, s, d).wait_send()
+
+    def fold_left(d, carry):
+        fold(d).wait_send()
+        return carry
+
+    lax.fori_loop(1, nm, fold_left, 0)
+    for d in range(1, nv):
+        fold_vec(d).wait_send()
     for h in range(2):
         for r in range(NRUN):
             out_copy(h, r).wait()
+
+
+def write_out(filtered, ritz, out, stiff, massg, sem):
+    copy = pltpu.make_async_copy(filtered, out, sem)
+    copy.start()
+    width = stiff.shape[0]
+    stiff[...] = ritz[0:width]
+    massg[...] = ritz[width : 2 * width]
+    copy.wait()
 
 
 def shards(nm, nv, panel, orient, mass, stiff_diag, near_coupling, far_coupling):
     rows, columns = panel.shape
     blocks = stiff_diag.shape[0]
     width = 128 // nm
+    cols = 128 // nv
     anywhere = pl.BlockSpec(memory_space=pl.ANY)
     inside = pl.BlockSpec(memory_space=pltpu.VMEM)
     dma = pltpu.SemaphoreType.DMA
@@ -435,26 +457,42 @@
         dma((nv - 1, STEPS)), dma((nv - 1, STEPS)), dma((nv - 1, STEPS)), dma((nv - 1, STEPS)),
         dma((nm - 1,)), dma((nm - 1,)), dma((nv - 1,)), dma((nv - 1,)),
     ]
-    filtered, stiff, massg = pl.pallas_call(
+    filtered, ritz = pl.pallas_call(
         functools.partial(kernel, nm, nv),
         out_shape=(
             jax.ShapeDtypeStruct((columns, rows), F32),
-            jax.ShapeDtypeStruct((width, 128 // nv), F32),
-            jax.ShapeDtypeStruct((width, 128 // nv), F32),
+            jax.ShapeDtypeStruct((2 * width, cols), F32),
         ),
-        in_specs=[anywhere] * 6,
+        in_specs=[pl.BlockSpec(memory_space=pltpu.HBM)] * 6,
+        out_specs=(anywhere, inside),
+        scratch_shapes=scratch,
+        compiler_params=pltpu.CompilerParams(
+            collective_id=0, has_side_effects=True, vmem_limit_bytes=VMEM_LIMIT),
+        name="filter_ritz",
+    )(*[
+        pltpu.with_memory_space_constraint(a, pltpu.HBM)
+        for a in (
+            panel.T,
+            orient.reshape(blocks, BS),
+            mass.reshape(blocks, BS),
+            stiff_diag,
+            near_coupling,
+            far_coupling,
+        )
+    ])
+    filtered, stiff, massg = pl.pallas_call(
+        write_out,
+        out_shape=(
+            jax.ShapeDtypeStruct((columns, rows), F32),
+            jax.ShapeDtypeStruct((width, cols), F32),
+            jax.ShapeDtypeStruct((width, cols), F32),
+        ),
+        in_specs=[inside, inside],
         out_specs=(anywhere, inside, inside),
-        scratch_shapes=scratch,
-        compiler_params=pltpu.CompilerParams(collective_id=0, has_side_effects=True),
-        name="filter_ritz",
-    )(
-        panel.T,
-        orient.reshape(blocks, BS),
-        mass.reshape(blocks, BS),
-        stiff_diag,
-        near_coupling,
-        far_coupling,
-    )
+        scratch_shapes=[pltpu.SemaphoreType.DMA],
+        compiler_params=pltpu.CompilerParams(vmem_limit_bytes=VMEM_LIMIT),
+        name="write_out",
+    )(filtered, ritz)
     return (filtered.T, stiff.T, massg.T)
 
 

time: 70.3 us -> 66.6 us (0.947)
  local copies, waits for them, and re-layouts: 3.43 us -> 0 us
    unnamed x7 -> x0, local copies, waits for them, and re-layouts: 3.43 us -> none
    pallas_call x1, Pallas kernels: 66.1 us -> 64.3 us  [shards(): pl.pallas_call(functools.partial(kernel, nm, nv), out_shape=(jax.ShapeDty...]
    pallas_call x0 -> x1, Pallas kernels: none -> 1.56 us  [shards(): pl.pallas_call(write_out, out_shape=(jax.ShapeDtypeStruct((columns, rows)...]
where the time goes in v2:
time: 66.6 us; the launch traced here: 66.5 us
  Pallas kernels  65.8 us (99%)
    pallas_call x1, Pallas kernels, shards(): pl.pallas_call(functools.partial(kernel, nm, nv), out_shape=(jax.ShapeDty...  64.3 us
    pallas_call x1, Pallas kernels, shards(): pl.pallas_call(write_out, out_shape=(jax.ShapeDtypeStruct((columns, rows)...  1.56 us

profile of v2, /device:TPU:1, one launch (start us, length us, event | category | flops | bytes accessed | tf_op | source)
XLA Modules:
  0.0 66.5 jit_solution(5080815675828893382)
XLA Ops:
  0.6 64.3 %filter_ritz.1 = (f32[32,8192]{1,0:T(8,128)S(1)}, f32[8,32]{1,0:T(8,128)S(1)}) custom-call(f32[32,8192]{1,0:T(8,128)} %bitcast.6, s32[64,128]{1,0:T(8,128)} %bitcast.7, f32[64,128]{1,0:T(8,128)} %bitcast.8, bf16[64,128,128]{2,1,0:T(8,128)(2,1)} %diag_hbm.1, bf16[64,128,128]{2,1,0:T(8,128)(2,1)} %near_hbm.1, bf16[64,128,128]{2,1,0:T(8,128)(2,1)} %far_hbm.1), custom_call_target="tpu_custom_call" | custom-call | tf_op jit(solution)/shard_map/filter_ritz/pallas_call | solution.py:460
  64.9 1.6 %write_out.1 = (f32[32,8192]{1,0:T(8,128)}, f32[4,32]{1,0:T(4,128)}, f32[4,32]{1,0:T(4,128)}) custom-call(f32[32,8192]{1,0:T(8,128)S(1)} %get-tuple-element.8.filtered, f32[8,32]{1,0:T(8,128)S(1)} %get-tuple-element.9.ritz), custom_call_target="tpu_custom_call" | custom-call | tf_op jit(solution)/shard_map/write_out/pallas_call | solution.py:483

commit v3 on v2

--- a/solution.py
+++ b/solution.py
@@ -17,6 +17,9 @@
 HALF = SPAN
 STEPS = 4
 CH = HALF // STEPS
+GROUP = 8
+F_WAYS = (2, 1, 3)
+G_WAYS = (1, 3)
 VMEM_LIMIT = 32 * 1024 * 1024
 
 MESH = pl.DeviceIdType.MESH
@@ -114,19 +117,18 @@
 
     barrier = pltpu.get_barrier_semaphore()
 
-    def hello_mesh(d, carry):
-        pl.semaphore_signal(barrier, inc=1, device_id=(lax.rem(m + d, nm), v), device_id_type=MESH)
-        return carry
-
-    lax.fori_loop(1, nm, hello_mesh, 0)
-    for d in range(1, nv):
-        pl.semaphore_signal(barrier, inc=1, device_id=(m, lax.rem(v + d, nv)), device_id_type=MESH)
+    group, member, ngroup = lax.div(m, GROUP), lax.rem(m, GROUP), nm // GROUP
+    greeted = [(lax.rem(m + 1, nm), v), (lax.rem(m + nm - 1, nm), v)]
+    greeted += [(lax.rem(group + d, ngroup) * GROUP + member, v) for d in range(1, ngroup)]
+    greeted += [(m, lax.rem(v + d, nv)) for d in range(1, nv)]
+    for peer in greeted:
+        pl.semaphore_signal(barrier, inc=1, device_id=peer, device_id_type=MESH)
 
     cp_or.wait()
     cp_ma.wait()
     scale[...] = orient[...].astype(F32) / jnp.sqrt(mass[...])
 
-    pl.semaphore_wait(barrier, nm - 1 + nv - 1)
+    pl.semaphore_wait(barrier, len(greeted))
 
     def send_u(par, s):
         return pltpu.make_async_remote_copy(
@@ -264,8 +266,8 @@
             device_id_type=MESH,
         )
 
-    def spread(box, whole, ss, rs, s):
-        for d in (2, 1, 3):
+    def spread(box, whole, ss, rs, s, ways):
+        for d in ways:
             exchange(box, whole, ss, rs, s, d).start()
         whole[s, pl.ds(pl.multiple_of(32 * v, 32), 32), :] = box[s, v]
 
@@ -316,7 +318,7 @@
             start_u(nxt, s)
             start_p(nxt, s)
             if last:
-                spread(f_out, f_all, fs_sem, fr_sem, s)
+                spread(f_out, f_all, fs_sem, fr_sem, s, F_WAYS)
                 for r in runs_of(s):
                     out_copy(0, r).start()
                     out_copy(1, r).start()
@@ -335,18 +337,36 @@
             deal(q, row_scale(q) * upper_total(NOPS % 2, q), g_out)
         for p in range(s * CH, (s + 1) * CH):
             deal(p, row_scale(p) * lower_total(NOPS % 2, p), g_out)
-        spread(g_out, g_all, gs_sem, gr_sem, s)
+        spread(g_out, g_all, gs_sem, gr_sem, s, G_WAYS)
 
     for s in range(STEPS):
         for d in range(1, nv):
             exchange(f_out, f_all, fs_sem, fr_sem, s, d).wait_recv()
         part = dot(f_all[s], f_all[s], NT)
         q_buf[1] = part if s == 0 else q_buf[1] + part
-    for s in range(STEPS):
-        for d in range(1, nv):
-            exchange(g_out, g_all, gs_sem, gr_sem, s, d).wait_recv()
-        part = dot(g_all[s], f_all[s], NT)
-        q_buf[0] = part if s == 0 else q_buf[0] + part
+    span = 128 // nv
+    away = lax.rem(lax.broadcasted_iota(jnp.int32, (span, 128), 1) // span - v + nv, nv)
+    q_buf[0] = jnp.zeros((128, 128), F32)
+    own = jnp.zeros((span, span), F32)
+    for s in range(STEPS):
+        for j in range(nv):
+            own = own + dot(g_out[s, j], f_out[s, j], NT)
+
+    def group_rows(d):
+        return pl.ds(pl.multiple_of(span * lax.rem(v + d, nv), span), span)
+
+    for d, partners in ((0, (1, 2, 3)), (1, (2, 3)), (3, (2,))):
+        part = jnp.zeros((span, 128), F32)
+        for s in range(STEPS):
+            if d > 0:
+                exchange(g_out, g_all, gs_sem, gr_sem, s, nv - d).wait_recv()
+            part = part + dot(g_all[s, group_rows(d), :], f_all[s], NT)
+        keep = away == partners[0]
+        for other in partners[1:]:
+            keep = jnp.logical_or(keep, away == other)
+        q_buf[0, group_rows(d), :] = jnp.where(keep, part, 0.0)
+    q_buf[0] = q_buf[0] + q_buf[0].T
+    q_buf[0, group_rows(0), :] += jnp.where(away == 0, jnp.concatenate([own] * nv, axis=1), 0.0)
 
     width = 128 // nm
     for i in range(nm):
@@ -400,6 +420,7 @@
     for s in range(STEPS):
         for d in range(1, nv):
             exchange(f_out, f_all, fs_sem, fr_sem, s, d).wait_send()
+        for d in G_WAYS:
             exchange(g_out, g_all, gs_sem, gr_sem, s, d).wait_send()
 
     def fold_left(d, carry):

time: 66.6 us -> 64.4 us (0.967)
  Pallas kernels: 65.8 us -> 63.7 us
    pallas_call x1, Pallas kernels: 64.3 us -> 62.1 us  [shards(): pl.pallas_call(functools.partial(kernel, nm, nv), out_shape=(jax.ShapeDty...]
where the time goes in v3:
time: 64.4 us; the launch traced here: 64.3 us
  Pallas kernels  63.7 us (99%)
    pallas_call x1, Pallas kernels, shards(): pl.pallas_call(functools.partial(kernel, nm, nv), out_shape=(jax.ShapeDty...  62.1 us
    pallas_call x1, Pallas kernels, shards(): pl.pallas_call(write_out, out_shape=(jax.ShapeDtypeStruct((columns, rows)...  1.56 us

profile of v3, /device:TPU:1, one launch (start us, length us, event | category | flops | bytes accessed | tf_op | source)
XLA Modules:
  0.0 64.3 jit_solution(3347904270840506909)
XLA Ops:
  0.6 62.1 %filter_ritz.1 = (f32[32,8192]{1,0:T(8,128)S(1)}, f32[8,32]{1,0:T(8,128)S(1)}) custom-call(f32[32,8192]{1,0:T(8,128)} %bitcast.6, s32[64,128]{1,0:T(8,128)} %bitcast.7, f32[64,128]{1,0:T(8,128)} %bitcast.8, bf16[64,128,128]{2,1,0:T(8,128)(2,1)} %diag_hbm.1, bf16[64,128,128]{2,1,0:T(8,128)(2,1)} %near_hbm.1, bf16[64,128,128]{2,1,0:T(8,128)(2,1)} %far_hbm.1), custom_call_target="tpu_custom_call" | custom-call | tf_op jit(solution)/shard_map/filter_ritz/pallas_call | solution.py:481
  62.7 1.6 %write_out.1 = (f32[32,8192]{1,0:T(8,128)}, f32[4,32]{1,0:T(4,128)}, f32[4,32]{1,0:T(4,128)}) custom-call(f32[32,8192]{1,0:T(8,128)S(1)} %get-tuple-element.8.filtered, f32[8,32]{1,0:T(8,128)S(1)} %get-tuple-element.9.ritz), custom_call_target="tpu_custom_call" | custom-call | tf_op jit(solution)/shard_map/write_out/pallas_call | solution.py:504

commit v4 on v3

--- a/solution.py
+++ b/solution.py
@@ -384,16 +384,18 @@
             device_id_type=MESH,
         )
 
-    def fold_start(d, carry):
+    def hops(d):
+        chips = (d // GROUP, d % GROUP // 2)
+        return sum(min(c, 4 - c) for c in chips)
+
+    far_first = sorted(range(1, nm), key=hops, reverse=True)
+    for d in far_first:
         fold(d).start()
-        return carry
-
-    def fold_wait(d, carry):
+    total = t_buf[m]
+    for d in reversed(far_first):
         fold(d).wait_recv()
-        return carry + r_buf[d - 1]
-
-    lax.fori_loop(1, nm, fold_start, 0)
-    s_buf[...] = lax.fori_loop(1, nm, fold_wait, t_buf[m])
+        total = total + r_buf[d - 1]
+    s_buf[...] = total
 
     def fold_vec(d):
         return pltpu.make_async_remote_copy(

time: 64.4 us -> 64.3 us (level)
  no operation moved by 1% of the time
where the time goes in v4:
time: 64.3 us; the launch traced here: 63.9 us
  Pallas kernels  63.3 us (98%)
    pallas_call x1, Pallas kernels, shards(): pl.pallas_call(functools.partial(kernel, nm, nv), out_shape=(jax.ShapeDty...  61.7 us
    pallas_call x1, Pallas kernels, shards(): pl.pallas_call(write_out, out_shape=(jax.ShapeDtypeStruct((columns, rows)...  1.56 us

profile of v4, /device:TPU:1, one launch (start us, length us, event | category | flops | bytes accessed | tf_op | source)
XLA Modules:
  0.0 63.9 jit_solution(7900641982112083416)
XLA Ops:
  0.6 61.7 %filter_ritz.1 = (f32[32,8192]{1,0:T(8,128)S(1)}, f32[8,32]{1,0:T(8,128)S(1)}) custom-call(f32[32,8192]{1,0:T(8,128)} %bitcast.6, s32[64,128]{1,0:T(8,128)} %bitcast.7, f32[64,128]{1,0:T(8,128)} %bitcast.8, bf16[64,128,128]{2,1,0:T(8,128)(2,1)} %diag_hbm.1, bf16[64,128,128]{2,1,0:T(8,128)(2,1)} %near_hbm.1, bf16[64,128,128]{2,1,0:T(8,128)(2,1)} %far_hbm.1), custom_call_target="tpu_custom_call" | custom-call | tf_op jit(solution)/shard_map/filter_ritz/pallas_call | solution.py:483
  62.4 1.6 %write_out.1 = (f32[32,8192]{1,0:T(8,128)}, f32[4,32]{1,0:T(4,128)}, f32[4,32]{1,0:T(4,128)}) custom-call(f32[32,8192]{1,0:T(8,128)S(1)} %get-tuple-element.8.filtered, f32[8,32]{1,0:T(8,128)S(1)} %get-tuple-element.9.ritz), custom_call_target="tpu_custom_call" | custom-call | tf_op jit(solution)/shard_map/write_out/pallas_call | solution.py:506

commit v5 on v4

--- a/solution.py
+++ b/solution.py
@@ -15,7 +15,7 @@
 CENTER = 6.0
 
 HALF = SPAN
-STEPS = 4
+STEPS = 8
 CH = HALF // STEPS
 GROUP = 8
 F_WAYS = (2, 1, 3)
@@ -314,6 +314,8 @@
                 value = recur(p, lower_total(par, p), par, weight, fresh)
                 if last:
                     deal(p, value, f_out)
+            if s > 0:
+                local_step(s - 1)
             products_down(s)
             start_u(nxt, s)
             start_p(nxt, s)
@@ -322,7 +324,7 @@
                 for r in runs_of(s):
                     out_copy(0, r).start()
                     out_copy(1, r).start()
-            local_step(s)
+        local_step(STEPS - 1)
 
     def loop_body(k, carry):
         operation(k, False)

time: 64.3 us -> 63.5 us (0.988)
  no operation moved by 1% of the time
where the time goes in v5:
time: 63.5 us; the launch traced here: 63.4 us
  Pallas kernels  62.8 us (99%)
  between operations  0.64 us (1%)
    pallas_call x1, Pallas kernels, shards(): pl.pallas_call(functools.partial(kernel, nm, nv), out_shape=(jax.ShapeDty...  61.2 us
    pallas_call x1, Pallas kernels, shards(): pl.pallas_call(write_out, out_shape=(jax.ShapeDtypeStruct((columns, rows)...  1.56 us

profile of v5, /device:TPU:1, one launch (start us, length us, event | category | flops | bytes accessed | tf_op | source)
XLA Modules:
  0.0 63.4 jit_solution(15888347068895374496)
XLA Ops:
  0.6 61.2 %filter_ritz.1 = (f32[32,8192]{1,0:T(8,128)S(1)}, f32[8,32]{1,0:T(8,128)S(1)}) custom-call(f32[32,8192]{1,0:T(8,128)} %bitcast.6, s32[64,128]{1,0:T(8,128)} %bitcast.7, f32[64,128]{1,0:T(8,128)} %bitcast.8, bf16[64,128,128]{2,1,0:T(8,128)(2,1)} %diag_hbm.1, bf16[64,128,128]{2,1,0:T(8,128)(2,1)} %near_hbm.1, bf16[64,128,128]{2,1,0:T(8,128)(2,1)} %far_hbm.1), custom_call_target="tpu_custom_call" | custom-call | tf_op jit(solution)/shard_map/filter_ritz/pallas_call | solution.py:485
  61.8 1.6 %write_out.1 = (f32[32,8192]{1,0:T(8,128)}, f32[4,32]{1,0:T(4,128)}, f32[4,32]{1,0:T(4,128)}) custom-call(f32[32,8192]{1,0:T(8,128)S(1)} %get-tuple-element.8.filtered, f32[8,32]{1,0:T(8,128)S(1)} %get-tuple-element.9.ritz), custom_call_target="tpu_custom_call" | custom-call | tf_op jit(solution)/shard_map/write_out/pallas_call | solution.py:508
